TPU v7x, 32 devices: a whole 2x2x4 slice. The times are simulated.
32 devices in a mesh: inner: 8 (over z, y), cols: 4 (over x, core).
Axes of the slice: x: 2, y: 2, z: 4, core: 2. Of those that a mesh axis runs over, the one named last changes fastest.
Arguments:
- left_u: bfloat16 [64, 512, 128], P(('inner', 'cols')), may hold values from -6 to 6
- left_v: bfloat16 [64, 512, 128], P(('inner', 'cols')), may hold values from -0.0234375 to 0.0234375
- right_u: bfloat16 [16, 64, 512, 128], P('cols', 'inner'), may hold values from -6 to 6
- right_v: bfloat16 [16, 64, 512, 128], P('cols', 'inner'), may hold values from -0.1875 to 0.1875
- sketch: bfloat16 [16, 512, 128], P('cols'), may hold values from -0.25 to 0.25
- tile_index: int32 [16, 64], P('cols', 'inner'), may hold values from 0 to 63, as said below
- slot_mask: int32 [16, 64], P('cols', 'inner'), may hold values from 0 to 1, as said below
Outputs:
- basis: float32 [16, 512, 128], P('cols', 'inner')
- coeff: float32 [16, 512, 128], P('cols', 'inner')
Inputs may be any that keep to these rules, and one draw needn't show every extreme that they name: `tile_index`: slot s of an output tile belongs to inner group g = s // 8 and names a left tile of that group, g * 8 to g * 8 + 7; the tiles named by one output tile's slots of one group are distinct. `slot_mask`: in each output tile and inner group the live slots come first and there is at least one; in every output tile some group has all 8 slots live, and the others at most 4.
All inputs are finite; a program needn't handle non-finite values.
Results may differ from a plain program's by a relative error of at most 0.0045.
Values may be sent and summed in bfloat16 or wider, within the bound.
A program may use at most 64 MiB of HBM per device.

v0:
```python
import functools
import math

import jax
import jax.numpy as jnp
from jax import lax
from jax.experimental import pallas as pl
from jax.experimental.pallas import tpu as pltpu
from jax.sharding import PartitionSpec as P

MESH = pl.DeviceIdType.MESH
F32 = jnp.float32
BF16 = jnp.bfloat16
NN = (((1,), (0,)), ((), ()))
NT = (((1,), (1,)), ((), ()))
TN = (((0,), (0,)), ((), ()))


def mm(a, b, dims):
    return lax.dot_general(a, b, dims, preferred_element_type=F32)


def split(a):
    hi = a.astype(BF16)
    return hi, (a - hi.astype(F32)).astype(BF16)


def mm_f32(a, b, dims):
    return lax.dot_general(a, b, dims, precision=lax.Precision.HIGHEST, preferred_element_type=F32)


def kernel(
    n_in, n_co, left_u, left_v, right_u, right_v, sketch, index, mask, basis, coeff,
    ug, vg, vt, ru, rv, sk, phi, plo, mix, ybuf, sbuf, r1, s2f, s2b, r2, yrow, yb,
    cbuf, csbuf, cr1, cs2f, cs2b, cr2, crow, xm, scale, bt,
    load_sem, gs_sem, gr_sem, rs_send, rs_recv, ag_send, ag_recv,
):
    nx = n_co // 2
    ny = nx
    nz = n_in // ny
    tpd = left_u.shape[0]
    tiles = tpd * n_co
    n_out, slots, nb, rk = right_u.shape
    rows = nb // n_in
    me_in = lax.axis_index("inner")
    me_co = lax.axis_index("cols")
    x, core = lax.div(me_co, 2), lax.rem(me_co, 2)
    z, y = lax.div(me_in, ny), lax.rem(me_in, ny)

    def co_at(dx):
        return lax.rem(x + dx, nx) * 2 + core

    partner = x * 2 + (1 - core)

    def z_at(dz):
        return lax.rem(z + dz, nz) * ny + y

    def y_at(dy):
        return z * ny + lax.rem(y + dy, ny)

    sends = []

    def remote(src, dst, s_sem, r_sem, **dev):
        return pltpu.make_async_remote_copy(
            src_ref=src, dst_ref=dst, send_sem=s_sem, recv_sem=r_sem,
            device_id=dev, device_id_type=MESH,
        )

    def go(copy):
        copy.start()
        sends.append(copy)

    loads = []
    for j in range(n_out):
        for num, (src, dst) in enumerate(((sketch, sk), (right_v, rv), (right_u, ru))):
            loads.append(pltpu.make_async_copy(src.at[j], dst.at[j], load_sem.at[j, num]))
    own = pl.ds(me_co * tpd, tpd)
    own_v = pltpu.make_async_copy(left_v, vg.at[own], load_sem.at[n_out, 0])
    own_u = pltpu.make_async_copy(left_u, ug.at[own], load_sem.at[n_out, 1])
    for c in [own_v, own_u] + loads:
        c.start()

    barrier = pltpu.get_barrier_semaphore()
    for dx in range(1, nx):
        pl.semaphore_signal(barrier, inc=1, device_id={"cols": co_at(dx)}, device_id_type=MESH)
    pl.semaphore_signal(barrier, inc=1, device_id={"cols": partner}, device_id_type=MESH)
    for dy in range(1, ny):
        pl.semaphore_signal(barrier, inc=1, device_id={"inner": y_at(dy)}, device_id_type=MESH)
    for dz in range(1, nz):
        pl.semaphore_signal(barrier, inc=1, device_id={"inner": z_at(dz)}, device_id_type=MESH)
    pl.semaphore_wait(barrier, nx - 1 + 1 + ny - 1 + nz - 1)

    for num, (src, dst) in enumerate(((left_v, vg), (left_u, ug))):
        for dx in range(1, nx):
            go(remote(src, dst.at[own], gs_sem.at[num, dx], gr_sem.at[num, dx], cols=co_at(dx)))
        go(remote(src, dst.at[own], gs_sem.at[num, 0], gr_sem.at[num, 0], cols=partner))

    def block(dst, position):
        return dst.at[pl.ds(position * tpd, tpd)]

    def forward(num, dst):
        for dx in range(1, nx):
            part = block(dst, co_at(nx - dx))
            remote(part, part, gs_sem.at[num, dx], gr_sem.at[num, dx], cols=partner).wait_recv()
            go(remote(part, part, gs_sem.at[num, nx + dx], gr_sem.at[num, nx + dx], cols=partner))

    def gathered(num, dst):
        part = block(dst, partner)
        remote(part, part, gs_sem.at[num, 0], gr_sem.at[num, 0], cols=partner).wait_recv()
        for dx in range(1, nx):
            part = block(dst, lax.rem(x + nx - dx, nx) * 2 + (1 - core))
            remote(part, part, gs_sem.at[num, nx + dx], gr_sem.at[num, nx + dx], cols=partner).wait_recv()

    for c in loads:
        c.wait()
    forward(0, vg)
    gathered(0, vg)
    own_v.wait()
    own_u.wait()

    @pl.loop(0, tiles)
    def _(t):
        vt[t] = jnp.transpose(vg[t])

    for j in range(n_out):
        om = jnp.transpose(sk[j])

        @pl.loop(0, slots // 4)
        def _(quad, j=j, om=om):
            for s in [quad * 4 + i for i in range(4)]:
                live = mask[j, s].astype(F32)
                probe_hi, probe_lo = split(mm(om, rv[j, s], NN))
                pair_hi, pair_lo = split(mm(vt[lax.rem(index[j, s], tiles)], ru[j, s], NN))
                phi[j, s] = pair_hi
                plo[j, s] = pair_lo
                mixed = mm(pair_hi, probe_hi, NT) + mm(pair_hi, probe_lo, NT) + mm(pair_lo, probe_hi, NT)
                mix[j, s] = (mixed * live).astype(BF16)

        if j == 0:
            forward(1, ug)

    gathered(1, ug)

    def scatter_first(phase, j, total, buf, sb, first):
        buf[j] = total.reshape(nz, ny, rows, rk)
        low = total.astype(BF16).reshape(nz, ny, rows, rk)
        for yy in range(ny):
            sb[j, yy] = low[:, yy]
        for dy in range(1, ny):
            go(remote(
                sb.at[j, lax.rem(y + dy, ny)], first.at[j, dy],
                rs_send.at[phase, j, dy], rs_recv.at[phase, j, dy], inner=y_at(dy),
            ))

    def scatter_second(phase, j, buf, sb, first, sumf, sumb, second):
        total = buf[j, :, y]
        for dy in range(1, ny):
            part = first.at[j, dy]
            remote(part, part, rs_send.at[phase, j, dy], rs_recv.at[phase, j, dy], inner=y_at(dy)).wait_recv()
            total = total + first[j, dy].astype(F32)
        sumf[j] = total
        sumb[j] = total.astype(BF16)
        for dz in range(1, nz):
            go(remote(
                sumb.at[j, lax.rem(z + dz, nz)], second.at[j, dz],
                rs_send.at[phase, j, ny + dz], rs_recv.at[phase, j, ny + dz], inner=z_at(dz),
            ))

    def scatter_last(phase, j, sumf, second):
        total = sumf[j, z]
        for dz in range(1, nz):
            part = second.at[j, dz]
            remote(part, part, rs_send.at[phase, j, ny + dz], rs_recv.at[phase, j, ny + dz], inner=z_at(dz)).wait_recv()
            total = total + second[j, dz].astype(F32)
        return total

    for j in range(n_out):
        total = mm(ug[lax.rem(index[j, 0], tiles)], mix[j, 0], NN)
        for s in range(1, slots):
            total = total + mm(ug[lax.rem(index[j, s], tiles)], mix[j, s], NN)
        scatter_first(0, j, total, ybuf, sbuf, r1)
    for j in range(n_out):
        scatter_second(0, j, ybuf, sbuf, r1, s2f, s2b, r2)

    for j in range(n_out):
        total = scatter_last(0, j, s2f, r2)
        yrow[j] = total
        yb[j, me_in] = total.astype(BF16)
        part = yb.at[j, me_in]
        for dz in range(1, nz):
            go(remote(part, part, ag_send.at[j, 0, dz], ag_recv.at[j, 0, dz], inner=z_at(dz)))
        for dy in range(1, ny):
            go(remote(part, part, ag_send.at[j, dy, 0], ag_recv.at[j, dy, 0], inner=y_at(dy)))
    for j in range(n_out):
        for dz in range(1, nz):
            part = yb.at[j, z_at(nz - dz)]
            remote(part, part, ag_send.at[j, 0, dz], ag_recv.at[j, 0, dz], inner=z_at(dz)).wait_recv()
            for dy in range(1, ny):
                go(remote(part, part, ag_send.at[j, dy, dz], ag_recv.at[j, dy, dz], inner=y_at(dy)))

    for j in range(n_out):
        for dy in range(1, ny):
            for dz in range(nz):
                pos = lax.rem(z + nz - dz, nz) * ny + lax.rem(y + ny - dy, ny)
                part = yb.at[j, pos]
                remote(part, part, ag_send.at[j, dy, dz], ag_recv.at[j, dy, dz], inner=y_at(dy)).wait_recv()
        summed_t = jnp.transpose(yb[j].reshape(nb, rk))

        @pl.loop(0, slots // 4)
        def _(quad, j=j, summed_t=summed_t):
            for s in [quad * 4 + i for i in range(4)]:
                live = mask[j, s].astype(F32)
                z_hi, z_lo = split(mm(summed_t, ug[lax.rem(index[j, s], tiles)], NN))
                back = mm(z_hi, phi[j, s], NN) + mm(z_hi, plo[j, s], NN) + mm(z_lo, phi[j, s], NN)
                b_hi, b_lo = split(back * live)
                bt[j, s, :rk] = b_hi
                bt[j, s, rk:] = b_lo

        wide = mm(rv[j, 0], bt[j, 0], NT)
        for s in range(1, slots):
            wide = wide + mm(rv[j, s], bt[j, s], NT)
        total = wide[:, :rk] + wide[:, rk:]
        scatter_first(1, j, total, cbuf, csbuf, cr1)

    row_id = lax.broadcasted_iota(jnp.int32, (rk, rk), 0)
    col_id = lax.broadcasted_iota(jnp.int32, (rk, rk), 1)
    for j in range(n_out):
        summed = yb[j].reshape(nb, rk)
        gram = mm(summed, summed, TN)
        diag = jnp.where(row_id == col_id, gram, 0.0)
        s_row = lax.rsqrt(jnp.sum(diag, axis=0, keepdims=True))
        s_col = lax.rsqrt(jnp.sum(diag, axis=1, keepdims=True))
        scale[j] = s_row
        xm[j] = gram * s_col * s_row

    sub8 = lax.broadcasted_iota(jnp.int32, (8, rk), 0)
    lane8 = lax.broadcasted_iota(jnp.int32, (8, rk), 1)

    def eliminate(start, stop):
        @pl.loop(start, stop)
        def _(b):
            base = pl.multiple_of(b * 8, 8)
            near = lane8 - base
            at = pl.ds(base, 8)
            slabs = [xm[j, at] for j in range(n_out)]
            cols = [
                [
                    jnp.broadcast_to(jnp.sum(jnp.where(near == i, slab, 0.0), axis=1, keepdims=True), (8, rk))
                    for i in range(8)
                ]
                for slab in slabs
            ]
            pivots = [jnp.ones((8, rk), F32)] * n_out
            for k in range(8):
                hot = jnp.where(near[:1] == k, 1.0, 0.0)
                for j in range(n_out):
                    column = cols[j][k]
                    pivots[j] = jnp.where(sub8 == k, column[k : k + 1], pivots[j])
                    weight = jnp.where(sub8 > k, column * (1.0 / column[k : k + 1]), 0.0)
                    slabs[j] = slabs[j] - weight * (slabs[j][k : k + 1] + hot)
                    for i in range(k + 1, 8):
                        cols[j][i] = cols[j][i] - weight * cols[j][i][k : k + 1]
            for j in range(n_out):
                ahead = jnp.where(near >= 8, slabs[j] / pivots[j], 0.0)
                unit = jnp.where(near == sub8, 1.0, jnp.where((near >= 0) & (near > sub8) & (near < 8), 0.0, slabs[j]))
                near_all = col_id - base
                clear = (row_id - base >= 8) & (near_all >= 0) & (near_all < 8)
                xm[j] = jnp.where(clear, 0.0, xm[j]) - mm_f32(ahead, unit, TN)
                xm[j, at] = slabs[j]

    blocks = rk // 8
    eliminate(0, blocks // 2)
    for j in range(n_out):
        scatter_second(1, j, cbuf, csbuf, cr1, cs2f, cs2b, cr2)
    eliminate(blocks // 2, blocks)

    for j in range(n_out):
        work = xm[j]
        pivots = jnp.sum(jnp.where(row_id == col_id, work, 0.0), axis=1, keepdims=True)
        lower = jnp.where(col_id < row_id, work, jnp.where(row_id == col_id, 1.0, 0.0))
        inverse = lower * lax.rsqrt(pivots) * scale[j]
        basis[j] = mm_f32(yrow[j], inverse, NT) * math.sqrt(nb)
        coeff[j] = mm_f32(scatter_last(1, j, cs2f, cr2), inverse, NT)

    for copy in sends:
        copy.wait_send()


def body(n_in, n_co, left_u, left_v, right_u, right_v, sketch, tile_index, slot_mask):
    n_out, slots, nb, rk = right_u.shape
    tiles = left_u.shape[0] * n_co
    nx = n_co // 2
    ny = nx
    nz = n_in // ny
    rows = nb // n_in
    wire = [
        pltpu.VMEM((n_out, nz, ny, rows, rk), F32),
        pltpu.VMEM((n_out, ny, nz, rows, rk), BF16),
        pltpu.VMEM((n_out, ny, nz, rows, rk), BF16),
        pltpu.VMEM((n_out, nz, rows, rk), F32),
        pltpu.VMEM((n_out, nz, rows, rk), BF16),
        pltpu.VMEM((n_out, nz, rows, rk), BF16),
        pltpu.VMEM((n_out, rows, rk), F32),
    ]
    out = jax.ShapeDtypeStruct((n_out, rows, rk), F32)
    hbm = pl.BlockSpec(memory_space=pl.ANY)
    smem = pl.BlockSpec(memory_space=pltpu.SMEM)
    vmem = pl.BlockSpec(memory_space=pltpu.VMEM)
    return pl.pallas_call(
        functools.partial(kernel, n_in, n_co),
        out_shape=(out, out),
        in_specs=[hbm] * 5 + [smem] * 2,
        out_specs=(vmem, vmem),
        scratch_shapes=[
            pltpu.VMEM((tiles, nb, rk), BF16),
            pltpu.VMEM((tiles, nb, rk), BF16),
            pltpu.VMEM((tiles, rk, nb), BF16),
            pltpu.VMEM((n_out, slots, nb, rk), BF16),
            pltpu.VMEM((n_out, slots, nb, rk), BF16),
            pltpu.VMEM((n_out, nb, rk), BF16),
            pltpu.VMEM((n_out, slots, rk, rk), BF16),
            pltpu.VMEM((n_out, slots, rk, rk), BF16),
            pltpu.VMEM((n_out, slots, rk, rk), BF16),
        ]
        + wire
        + [pltpu.VMEM((n_out, n_in, rows, rk), BF16)]
        + wire
        + [
            pltpu.VMEM((n_out, rk, rk), F32),
            pltpu.VMEM((n_out, 1, rk), F32),
            pltpu.VMEM((n_out, slots, 2 * rk, rk), BF16),
            pltpu.SemaphoreType.DMA((n_out + 1, 3)),
            pltpu.SemaphoreType.DMA((2, 2 * nx)),
            pltpu.SemaphoreType.DMA((2, 2 * nx)),
            pltpu.SemaphoreType.DMA((2, n_out, ny + nz)),
            pltpu.SemaphoreType.DMA((2, n_out, ny + nz)),
            pltpu.SemaphoreType.DMA((n_out, ny, nz)),
            pltpu.SemaphoreType.DMA((n_out, ny, nz)),
        ],
        compiler_params=pltpu.CompilerParams(
            collective_id=0, has_side_effects=True, vmem_limit_bytes=60 * 1024 * 1024
        ),
    )(left_u, left_v, right_u, right_v, sketch, tile_index, slot_mask)


def solution(mesh):
    return jax.shard_map(
        functools.partial(body, mesh.shape["inner"], mesh.shape["cols"]),
        mesh=mesh,
        in_specs=(
            P(("inner", "cols"), None, None),
            P(("inner", "cols"), None, None),
            P("cols", "inner", None, None),
            P("cols", "inner", None, None),
            P("cols", None, None),
            P("cols", "inner"),
            P("cols", "inner"),
        ),
        out_specs=(P("cols", "inner", None), P("cols", "inner", None)),
        check_vma=False,
    )
```

profile of v0, /device:TPU:0, one launch (start us, length us, event | category | flops | bytes accessed | tf_op | source)
XLA Modules:
  0.0 72.6 jit_solution(13227631234214824276)
XLA Ops:
  0.6 68.8 %shard_map.86 = (f32[4,64,128]{2,1,0:T(8,128)}, f32[4,64,128]{2,1,0:T(8,128)}) custom-call(bf16[2,512,128]{2,1,0:T(8,128)(2,1)} %left_u.1, bf16[2,512,128]{2,1,0:T(8,128)(2,1)} %left_v.1, bf16[4,8,512,128]{3,2,1,0:T(8,128)(2,1)} %right_u.1, bf16[4,8,512,128]{3,2,1,0:T(8,128)(2,1)} %right_v.1, bf16[4,512,128]{2,1,0:T(8,128)(2,1)} %sketch.1, s32[4,8]{1,0:T(4,128)} %index.1, ...), custom_call_target="tpu_custom_call" | custom-call | tf_op jit(solution)/shard_map/pallas_call | solution.py:309
  69.5 1.6 %copy.11 = f32[4,64,128]{2,1,0:T(8,128)} copy(f32[4,64,128]{2,1,0:T(8,128)} %get-tuple-element.4) | data formatting | bytes 262144
  71.0 1.6 %copy.12 = f32[4,64,128]{2,1,0:T(8,128)} copy(f32[4,64,128]{2,1,0:T(8,128)} %get-tuple-element.5) | data formatting | bytes 262144
where the time goes:
time: 72.8 us; the launch traced here: 72.6 us
  Pallas kernels  68.8 us (95%)
  local copies, waits for them, and re-layouts  3.14 us (4%)
    pallas_call x1, Pallas kernels, body(): pl.pallas_call(functools.partial(kernel, n_in, n_co), out_shape=(out, out...  68.8 us
    unnamed x2, local copies, waits for them, and re-layouts  3.14 us

commit v1 on v0

v1 whole, which is shorter than its diff:
```python
import functools
import math

import jax
import jax.numpy as jnp
from jax import lax
from jax.experimental import pallas as pl
from jax.experimental.pallas import tpu as pltpu
from jax.sharding import PartitionSpec as P

MESH = pl.DeviceIdType.MESH
F32 = jnp.float32
BF16 = jnp.bfloat16
NN = (((1,), (0,)), ((), ()))
NT = (((1,), (1,)), ((), ()))
TN = (((0,), (0,)), ((), ()))


def mm(a, b, dims):
    return lax.dot_general(a, b, dims, preferred_element_type=F32)


def split(a):
    hi = a.astype(BF16)
    return hi, (a - hi.astype(F32)).astype(BF16)


def mm_f32(a, b, dims):
    return lax.dot_general(a, b, dims, precision=lax.Precision.HIGHEST, preferred_element_type=F32)


def wide(parts):
    return jnp.concatenate(parts, axis=1)


def kernel(
    n_in, n_co, left_u, left_v, right_u, right_v, sketch, index, mask, basis, coeff,
    ug, vg, ru, rv, sk, skt, inv, lv, pb, pk, mix, wt, ct,
    ybuf, sbuf, r1, s2f, s2b, r2, yrow, yb,
    cbuf, csbuf, cr1, cs2f, cs2b, cr2, xm, scale,
    load_sem, vs_sem, vr_sem, us_sem, ur_sem, rs_send, rs_recv, ag_send, ag_recv,
):
    nx = n_co // 2
    ny = nx
    nz = n_in // ny
    tpd, nb, rk = left_v.shape
    nch, part_rows = ug.shape[0], ug.shape[3]
    tiles = tpd * n_co
    n_out, slots = right_u.shape[:2]
    rows = nb // n_in
    me_in = lax.axis_index("inner")
    me_co = lax.axis_index("cols")
    x, core = lax.div(me_co, 2), lax.rem(me_co, 2)
    z, y = lax.div(me_in, ny), lax.rem(me_in, ny)
    def co_at(dx):
        return lax.rem(x + dx, nx) * 2 + core

    partner = x * 2 + (1 - core)

    def z_at(dz):
        return lax.rem(z + dz, nz) * ny + y

    def y_at(dy):
        return z * ny + lax.rem(y + dy, ny)

    sends = []

    def remote(src, dst, s_sem, r_sem, **dev):
        return pltpu.make_async_remote_copy(
            src_ref=src, dst_ref=dst, send_sem=s_sem, recv_sem=r_sem,
            device_id=dev, device_id_type=MESH,
        )

    def go(copy):
        copy.start()
        sends.append(copy)

    own = pl.ds(me_co * tpd, tpd)
    early, late = [], []
    for j in range(n_out):
        early.append(pltpu.make_async_copy(sketch.at[j], sk.at[j], load_sem.at[j, 0]))
        early.append(pltpu.make_async_copy(right_v.at[j], rv.at[j], load_sem.at[j, 1]))
    late.append(pltpu.make_async_copy(left_v, vg.at[own], load_sem.at[n_out, 0]))
    for j in range(n_out):
        late.append(pltpu.make_async_copy(right_u.at[j], ru.at[j], load_sem.at[j, 2]))
    own_u = [
        pltpu.make_async_copy(left_u.at[:, :, c], ug.at[c, own], load_sem.at[n_out + 1, c]) for c in range(nch)
    ]
    for copy in early + late + own_u:
        copy.start()

    barrier = pltpu.get_barrier_semaphore()
    for dx in range(1, nx):
        pl.semaphore_signal(barrier, inc=1, device_id={"cols": co_at(dx)}, device_id_type=MESH)
    pl.semaphore_signal(barrier, inc=1, device_id={"cols": partner}, device_id_type=MESH)
    for dy in range(1, ny):
        pl.semaphore_signal(barrier, inc=1, device_id={"inner": y_at(dy)}, device_id_type=MESH)
    for dz in range(1, nz):
        pl.semaphore_signal(barrier, inc=1, device_id={"inner": z_at(dz)}, device_id_type=MESH)
    pl.semaphore_wait(barrier, nx - 1 + 1 + ny - 1 + nz - 1)

    for i in range(tpd):
        to = vg.at[me_co * tpd + i]
        for dx in range(1, nx):
            go(remote(left_v.at[i], to, vs_sem.at[i, dx], vr_sem.at[i, dx], cols=co_at(dx)))
        go(remote(left_v.at[i], to, vs_sem.at[i, 0], vr_sem.at[i, 0], cols=partner))
    for c in range(nch):
        for dx in range(1, nx):
            go(remote(left_u.at[:, :, c], ug.at[c, own], us_sem.at[c, dx], ur_sem.at[c, dx], cols=co_at(dx)))
        go(remote(left_u.at[:, :, c], ug.at[c, own], us_sem.at[c, 0], ur_sem.at[c, 0], cols=partner))

    def arrived(part, s_sem, r_sem):
        remote(part, part, s_sem, r_sem, cols=partner).wait_recv()

    for j in range(n_out):
        named = [lax.rem(index[j, s], tiles) for s in range(slots)]
        alive = [mask[j, s] for s in range(slots)]
        for k in range(tiles):
            at, live = jnp.int32(0), jnp.int32(0)
            for s in range(slots):
                hit = named[s] == k
                at = jnp.where(hit, s, at)
                live = jnp.where(hit, alive[s], live)
            inv[j, k] = at
            lv[j, k] = live

    for copy in early:
        copy.wait()

    @pl.loop(0, n_out)
    def _(j):
        skt[...] = jnp.transpose(sk[j])
        for s in range(0, slots, 2):
            out = mm(skt[...], wide([rv[j, s], rv[j, s + 1]]), NN)
            for i in range(2):
                hi, lo = split(out[:, i * rk : (i + 1) * rk])
                pb[j, s + i, :rk] = hi
                pb[j, s + i, rk:] = lo

    for copy in late:
        copy.wait()

    def pair(k):
        vt = jnp.transpose(vg[k])
        for first in range(0, n_out, 2):
            js = (first, first + 1)
            at = [inv[j, k] for j in js]
            out = mm(vt, wide([ru[j, s] for j, s in zip(js, at)]), NN)
            for i, (j, s) in enumerate(zip(js, at)):
                hi, lo = split(out[:, i * rk : (i + 1) * rk] * lv[j, k].astype(F32))
                both = wide([hi, lo])
                pk[j, k] = both
                probe = pb[j, s]
                mixed = mm(both, wide([probe, probe]), NT)
                mix[k, :, j * rk : (j + 1) * rk] = (mixed[:, :rk] + mixed[:, rk:]).astype(BF16)

    def fold(base):
        @pl.loop(0, tpd)
        def _(i):
            k = base + i
            for j in range(n_out):
                right = rv[j, inv[j, k]]
                hi, lo = split(mm(wide([right, right]), pk[j, k], NT))
                wt[j, k, 0] = hi
                wt[j, k, 1] = lo

    for i in range(tpd):
        pair(me_co * tpd + i)
    for i in range(tpd):
        k = partner * tpd + i
        arrived(vg.at[k], vs_sem.at[i, 0], vr_sem.at[i, 0])
        pair(k)

    def pass_on_v(i):
        for dx in range(1, nx):
            k = co_at(nx - dx) * tpd + i
            arrived(vg.at[k], vs_sem.at[i, dx], vr_sem.at[i, dx])
            go(remote(vg.at[k], vg.at[k], vs_sem.at[i, nx + dx], vr_sem.at[i, nx + dx], cols=partner))

    fold(me_co * tpd)
    for i in range(tpd):
        pass_on_v(i)
        for dx in range(1, nx):
            pair(co_at(nx - dx) * tpd + i)
        if i == tpd - 1:
            fold(partner * tpd)
        for dx in range(1, nx):
            k = (lax.rem(x + nx - dx, nx) * 2 + (1 - core)) * tpd + i
            arrived(vg.at[k], vs_sem.at[i, nx + dx], vr_sem.at[i, nx + dx])
            pair(k)
    for dx in range(1, nx):
        fold(co_at(nx - dx) * tpd)
    for copy in own_u:
        copy.wait()

    def block_u(c, position):
        return ug.at[c, pl.ds(position * tpd, tpd)]

    def pass_on_u(c):
        for dx in range(1, nx):
            part = block_u(c, co_at(nx - dx))
            arrived(part, us_sem.at[c, dx], ur_sem.at[c, dx])
            go(remote(part, part, us_sem.at[c, nx + dx], ur_sem.at[c, nx + dx], cols=partner))

    def gathered_u(c):
        arrived(block_u(c, partner), us_sem.at[c, 0], ur_sem.at[c, 0])
        for dx in range(1, nx):
            part = block_u(c, lax.rem(x + nx - dx, nx) * 2 + (1 - core))
            arrived(part, us_sem.at[c, nx + dx], ur_sem.at[c, nx + dx])

    def chunk_u(c):
        return wide([ug[c, k].reshape(nb // nch, rk) for k in range(tiles)])

    def scatter_first(phase, j, total, buf, sb, first):
        shape = (nz, ny, total.shape[0] // n_in, rk)
        buf[j] = total.reshape(shape)
        low = total.astype(BF16).reshape(shape)
        for yy in range(ny):
            sb[j, yy] = low[:, yy]
        for dy in range(1, ny):
            go(remote(
                sb.at[j, lax.rem(y + dy, ny)], first.at[j, dy],
                rs_send.at[phase, j, dy], rs_recv.at[phase, j, dy], inner=y_at(dy),
            ))

    def scatter_second(phase, j, buf, sb, first, sumf, sumb, second):
        total = buf[j, :, y]
        for dy in range(1, ny):
            part = first.at[j, dy]
            remote(part, part, rs_send.at[phase, j, dy], rs_recv.at[phase, j, dy], inner=y_at(dy)).wait_recv()
            total = total + first[j, dy].astype(F32)
        sumf[j] = total
        sumb[j] = total.astype(BF16)
        for dz in range(1, nz):
            go(remote(
                sumb.at[j, lax.rem(z + dz, nz)], second.at[j, dz],
                rs_send.at[phase, j, ny + dz], rs_recv.at[phase, j, ny + dz], inner=z_at(dz),
            ))

    def scatter_last(phase, j, sumf, second):
        total = sumf[j, z]
        for dz in range(1, nz):
            part = second.at[j, dz]
            remote(part, part, rs_send.at[phase, j, ny + dz], rs_recv.at[phase, j, ny + dz], inner=z_at(dz)).wait_recv()
            total = total + second[j, dz].astype(F32)
        return total

    def sketched(c):
        mixed = mix[...]
        mixed = mixed.reshape(tiles * rk, n_out * rk)
        total = mm(chunk_u(c), mixed, NN)
        for j in range(n_out):
            scatter_first(c, j, total[:, j * rk : (j + 1) * rk], ybuf.at[c], sbuf.at[c], r1.at[c])

    def second(c, j):
        scatter_second(c, j, ybuf.at[c], sbuf.at[c], r1.at[c], s2f.at[c], s2b.at[c], r2.at[c])

    def last(c, j):
        total = scatter_last(c, j, s2f.at[c], r2.at[c])
        yrow[j, c * part_rows : (c + 1) * part_rows] = total
        yb[c, j, me_in] = total.astype(BF16)
        part = yb.at[c, j, me_in]
        for dz in range(1, nz):
            go(remote(part, part, ag_send.at[c, j, 0, dz], ag_recv.at[c, j, 0, dz], inner=z_at(dz)))
        for dy in range(1, ny):
            go(remote(part, part, ag_send.at[c, j, dy, 0], ag_recv.at[c, j, dy, 0], inner=y_at(dy)))

    def spread(c, j):
        for dz in range(1, nz):
            part = yb.at[c, j, z_at(nz - dz)]
            remote(part, part, ag_send.at[c, j, 0, dz], ag_recv.at[c, j, 0, dz], inner=z_at(dz)).wait_recv()
            for dy in range(1, ny):
                go(remote(part, part, ag_send.at[c, j, dy, dz], ag_recv.at[c, j, dy, dz], inner=y_at(dy)))

    def complete(c, j):
        for dy in range(1, ny):
            for dz in range(nz):
                pos = lax.rem(z + nz - dz, nz) * ny + lax.rem(y + ny - dy, ny)
                part = yb.at[c, j, pos]
                remote(part, part, ag_send.at[c, j, dy, dz], ag_recv.at[c, j, dy, dz], inner=y_at(dy)).wait_recv()

    def tile_t(j, c):
        left = wide([wt[j, k, h] for h in range(2) for k in range(tiles)])
        right = chunk_u(c)
        hi, lo = split(mm(left, wide([right, right]), NT))
        ct[j, c, 0] = hi
        ct[j, c, 1] = lo

    def y_of(j):
        return jnp.concatenate([yb[c, j].reshape(nb // nch, rk) for c in range(nch)], axis=0)

    def back(j):
        left = wide([ct[j, c, h] for h in range(2) for c in range(nch)])
        right = y_of(j)
        total = mm(left, jnp.concatenate([right, right], axis=0), NN)
        scatter_first(nch, j, total, cbuf, csbuf, cr1)

    work = [(j, c) for c in range(nch) for j in range(n_out)]

    def some(n):
        for _ in range(n):
            if work:
                tile_t(*work.pop(0))

    for dx in range(1, nx):
        fold((lax.rem(x + nx - dx, nx) * 2 + (1 - core)) * tpd)
    for c in range(nch):
        pass_on_u(c)
        gathered_u(c)
        sketched(c)
        if c < nch - 1:
            some(2)
    for c in range(nch):
        for j in range(n_out):
            second(c, j)
        some(2)
    for c in range(nch):
        for j in range(n_out):
            last(c, j)
        if c < nch - 1:
            some(2)
    some(len(work))
    for c in range(nch):
        for j in range(n_out):
            spread(c, j)
    for j in range(n_out):
        for c in range(nch):
            complete(c, j)
        back(j)

    row_id = lax.broadcasted_iota(jnp.int32, (rk, rk), 0)
    col_id = lax.broadcasted_iota(jnp.int32, (rk, rk), 1)
    for j in range(n_out):
        summed = y_of(j)
        gram = mm(summed, summed, TN)
        diag = jnp.where(row_id == col_id, gram, 0.0)
        s_row = lax.rsqrt(jnp.sum(diag, axis=0, keepdims=True))
        s_col = lax.rsqrt(jnp.sum(diag, axis=1, keepdims=True))
        scale[j] = s_row
        xm[j] = gram * s_col * s_row

    sub8 = lax.broadcasted_iota(jnp.int32, (8, rk), 0)
    lane8 = lax.broadcasted_iota(jnp.int32, (8, rk), 1)

    def eliminate(start, stop):
        @pl.loop(start, stop)
        def _(b):
            base = pl.multiple_of(b * 8, 8)
            near = lane8 - base
            at = pl.ds(base, 8)
            slabs = [xm[j, at] for j in range(n_out)]
            cols = [
                [
                    jnp.broadcast_to(jnp.sum(jnp.where(near == i, slab, 0.0), axis=1, keepdims=True), (8, rk))
                    for i in range(8)
                ]
                for slab in slabs
            ]
            pivots = [jnp.ones((8, rk), F32)] * n_out
            for k in range(8):
                hot = jnp.where(near[:1] == k, 1.0, 0.0)
                for j in range(n_out):
                    column = cols[j][k]
                    pivots[j] = jnp.where(sub8 == k, column[k : k + 1], pivots[j])
                    weight = jnp.where(sub8 > k, column * (1.0 / column[k : k + 1]), 0.0)
                    slabs[j] = slabs[j] - weight * (slabs[j][k : k + 1] + hot)
                    for i in range(k + 1, 8):
                        cols[j][i] = cols[j][i] - weight * cols[j][i][k : k + 1]
            for j in range(n_out):
                ahead = jnp.where(near >= 8, slabs[j] / pivots[j], 0.0)
                unit = jnp.where(near == sub8, 1.0, jnp.where((near >= 0) & (near > sub8) & (near < 8), 0.0, slabs[j]))
                near_all = col_id - base
                clear = (row_id - base >= 8) & (near_all >= 0) & (near_all < 8)
                xm[j] = jnp.where(clear, 0.0, xm[j]) - mm_f32(ahead, unit, TN)
                xm[j, at] = slabs[j]

    blocks = rk // 8
    done = 0
    for j in range(n_out):
        upto = min(blocks, blocks * (5 + 2 * j) // 16)
        eliminate(done, upto)
        done = upto
        scatter_second(nch, j, cbuf, csbuf, cr1, cs2f, cs2b, cr2)
    eliminate(done, blocks)

    for j in range(n_out):
        left = xm[j]
        pivots = jnp.sum(jnp.where(row_id == col_id, left, 0.0), axis=1, keepdims=True)
        lower = jnp.where(col_id < row_id, left, jnp.where(row_id == col_id, 1.0, 0.0))
        inverse = lower * lax.rsqrt(pivots) * scale[j]
        basis[j] = mm_f32(yrow[j], inverse, NT) * math.sqrt(nb)
        coeff[j] = mm_f32(scatter_last(nch, j, cs2f, cr2), inverse, NT)

    for copy in sends:
        copy.wait_send()


def body(n_in, n_co, left_u, left_v, right_u, right_v, sketch, tile_index, slot_mask):
    n_out, slots, nb, rk = right_u.shape
    tpd = left_u.shape[0]
    tiles = tpd * n_co
    nx = n_co // 2
    ny = nx
    nz = n_in // ny
    rows = nb // n_in
    nch = 2 if rows % 32 == 0 else 1
    part_rows = rows // nch

    def wire(lead, height):
        return [
            pltpu.VMEM((*lead, n_out, nz, ny, height, rk), F32),
            pltpu.VMEM((*lead, n_out, ny, nz, height, rk), BF16),
            pltpu.VMEM((*lead, n_out, ny, nz, height, rk), BF16),
            pltpu.VMEM((*lead, n_out, nz, height, rk), F32),
            pltpu.VMEM((*lead, n_out, nz, height, rk), BF16),
            pltpu.VMEM((*lead, n_out, nz, height, rk), BF16),
        ]

    out = jax.ShapeDtypeStruct((n_out, rows, rk), F32)
    hbm = pl.BlockSpec(memory_space=pl.ANY)
    smem = pl.BlockSpec(memory_space=pltpu.SMEM)
    vmem = pl.BlockSpec(memory_space=pltpu.VMEM)
    return pl.pallas_call(
        functools.partial(kernel, n_in, n_co),
        out_shape=(out, out),
        in_specs=[hbm] * 5 + [smem] * 2,
        out_specs=(vmem, vmem),
        scratch_shapes=[
            pltpu.VMEM((nch, tiles, n_in, part_rows, rk), BF16),
            pltpu.VMEM((tiles, nb, rk), BF16),
            pltpu.VMEM((n_out, slots, nb, rk), BF16),
            pltpu.VMEM((n_out, slots, nb, rk), BF16),
            pltpu.VMEM((n_out, nb, rk), BF16),
            pltpu.VMEM((rk, nb), BF16),
            pltpu.SMEM((n_out, tiles), jnp.int32),
            pltpu.SMEM((n_out, tiles), jnp.int32),
            pltpu.VMEM((n_out, slots, 2 * rk, rk), BF16),
            pltpu.VMEM((n_out, tiles, rk, 2 * rk), BF16),
            pltpu.VMEM((tiles, rk, n_out * rk), BF16),
            pltpu.VMEM((n_out, tiles, 2, nb, rk), BF16),
            pltpu.VMEM((n_out, nch, 2, nb, nb // nch), BF16),
        ]
        + wire((nch,), part_rows)
        + [pltpu.VMEM((n_out, rows, rk), F32), pltpu.VMEM((nch, n_out, n_in, part_rows, rk), BF16)]
        + wire((), rows)
        + [
            pltpu.VMEM((n_out, rk, rk), F32),
            pltpu.VMEM((n_out, 1, rk), F32),
            pltpu.SemaphoreType.DMA((n_out + 2, 3)),
            pltpu.SemaphoreType.DMA((tpd, 2 * nx)),
            pltpu.SemaphoreType.DMA((tpd, 2 * nx)),
            pltpu.SemaphoreType.DMA((nch, 2 * nx)),
            pltpu.SemaphoreType.DMA((nch, 2 * nx)),
            pltpu.SemaphoreType.DMA((nch + 1, n_out, ny + nz)),
            pltpu.SemaphoreType.DMA((nch + 1, n_out, ny + nz)),
            pltpu.SemaphoreType.DMA((nch, n_out, ny, nz)),
            pltpu.SemaphoreType.DMA((nch, n_out, ny, nz)),
        ],
        compiler_params=pltpu.CompilerParams(
            collective_id=0, has_side_effects=True, vmem_limit_bytes=60 * 1024 * 1024
        ),
    )(left_u.reshape(tpd, n_in, nch, part_rows, rk), left_v, right_u, right_v, sketch, tile_index, slot_mask)


def solution(mesh):
    return jax.shard_map(
        functools.partial(body, mesh.shape["inner"], mesh.shape["cols"]),
        mesh=mesh,
        in_specs=(
            P(("inner", "cols"), None, None),
            P(("inner", "cols"), None, None),
            P("cols", "inner", None, None),
            P("cols", "inner", None, None),
            P("cols", None, None),
            P("cols", "inner"),
            P("cols", "inner"),
        ),
        out_specs=(P("cols", "inner", None), P("cols", "inner", None)),
        check_vma=False,
    )
```

time: 72.8 us -> 61.6 us (0.85)
  Pallas kernels: 68.8 us -> 57.7 us
    pallas_call x1, Pallas kernels: 68.8 us -> 57.7 us  [body(): pl.pallas_call(functools.partial(kernel, n_in, n_co), out_shape=(out, out...]
where the time goes in v1:
time: 61.6 us; the launch traced here: 61.4 us
  Pallas kernels  57.7 us (94%)
  local copies, waits for them, and re-layouts  3.14 us (5%)
  between operations  0.64 us (1%)
    pallas_call x1, Pallas kernels, body(): pl.pallas_call(functools.partial(kernel, n_in, n_co), out_shape=(out, out...  57.7 us
    unnamed x2, local copies, waits for them, and re-layouts  3.14 us

profile of v1, /device:TPU:0, one launch (start us, length us, event | category | flops | bytes accessed | tf_op | source)
XLA Modules:
  0.0 61.4 jit_solution(10856252336314108657)
XLA Ops:
  0.6 57.7 %shard_map.86 = (f32[4,64,128]{2,1,0:T(8,128)}, f32[4,64,128]{2,1,0:T(8,128)}) custom-call(bf16[2,8,2,32,128]{4,3,2,1,0:T(8,128)(2,1)} %bitcast.1, bf16[2,512,128]{2,1,0:T(8,128)(2,1)} %left_v.1, bf16[4,8,512,128]{3,2,1,0:T(8,128)(2,1)} %right_u.1, bf16[4,8,512,128]{3,2,1,0:T(8,128)(2,1)} %right_v.1, bf16[4,512,128]{2,1,0:T(8,128)(2,1)} %sketch.1, ...), custom_call_target="tpu_custom_call" | custom-call | tf_op jit(solution)/shard_map/pallas_call | solution.py:423
  58.3 1.6 %copy.11 = f32[4,64,128]{2,1,0:T(8,128)} copy(f32[4,64,128]{2,1,0:T(8,128)} %get-tuple-element.4) | data formatting | bytes 262144
  59.9 1.6 %copy.12 = f32[4,64,128]{2,1,0:T(8,128)} copy(f32[4,64,128]{2,1,0:T(8,128)} %get-tuple-element.5) | data formatting | bytes 262144

commit v2 on v1

v2 whole, which is shorter than its diff:
```python
import functools
import math

import jax
import jax.numpy as jnp
from jax import lax
from jax.experimental import pallas as pl
from jax.experimental.pallas import tpu as pltpu
from jax.sharding import PartitionSpec as P

MESH = pl.DeviceIdType.MESH
F32 = jnp.float32
BF16 = jnp.bfloat16
NN = (((1,), (0,)), ((), ()))
NT = (((1,), (1,)), ((), ()))
TN = (((0,), (0,)), ((), ()))


def mm(a, b, dims):
    return lax.dot_general(a, b, dims, preferred_element_type=F32)


def split(a):
    hi = a.astype(BF16)
    return hi, (a - hi.astype(F32)).astype(BF16)


def mm_f32(a, b, dims):
    return lax.dot_general(a, b, dims, precision=lax.Precision.HIGHEST, preferred_element_type=F32)


def wide(parts):
    return jnp.concatenate(parts, axis=1)


def kernel(
    n_in, n_co, left_u, left_v, right_u, right_v, sketch, index_hbm, mask_hbm, outs,
    ug, vg, ru, rv, sk, skt, index, mask, inv, lv, pb, pk, mix, wt, ct,
    ybuf, sbuf, r1, s2f, s2b, r2, yrow, yb,
    cbuf, csbuf, cr1, cs2f, cs2b, cr2, xm, scale,
    load_sem, rv_sem, send_sem, v_sem, u_sem, sum_sem, ag_sem, back_sem,
):
    nx = n_co // 2
    ny = nx
    nz = n_in // ny
    tpd, nb, rk = left_v.shape
    nch, part_rows = ug.shape[0], ug.shape[3]
    groups = ct.shape[1]
    tiles = tpd * n_co
    n_out, slots = right_u.shape[:2]
    rows = nb // n_in
    me_in = lax.axis_index("inner")
    me_co = lax.axis_index("cols")
    x, core = lax.div(me_co, 2), lax.rem(me_co, 2)
    z, y = lax.div(me_in, ny), lax.rem(me_in, ny)
    def co_at(dx):
        return lax.rem(x + dx, nx) * 2 + core

    def other_at(dx):
        return lax.rem(x + dx, nx) * 2 + (1 - core)

    partner = other_at(0)

    def z_at(dz):
        return lax.rem(z + dz, nz) * ny + y

    def y_at(dy):
        return z * ny + lax.rem(y + dy, ny)

    V_OUT, U_OUT, SUM_Y, SUM_Z, GATHER, BACK_Y, BACK_Z = range(7)

    def remote(src, dst, kind, r_sem, **dev):
        return pltpu.make_async_remote_copy(
            src_ref=src, dst_ref=dst, send_sem=send_sem.at[kind], recv_sem=r_sem,
            device_id=dev, device_id_type=MESH,
        )

    def arrived(part, r_sem):
        pltpu.make_async_copy(part, part, r_sem).wait()

    own = pl.ds(me_co * tpd, tpd)
    tables = [pltpu.make_async_copy(index_hbm, index, load_sem.at[0]), pltpu.make_async_copy(mask_hbm, mask, load_sem.at[1])]
    first_sketch = pltpu.make_async_copy(sketch, sk, load_sem.at[2])
    rv_load = [pltpu.make_async_copy(right_v.at[j], rv.at[j], rv_sem.at[j]) for j in range(n_out)]
    own_v = pltpu.make_async_copy(left_v, vg.at[own], load_sem.at[3])
    ru_load = pltpu.make_async_copy(right_u, ru, load_sem.at[4])
    for copy in tables + [first_sketch] + rv_load + [own_v, ru_load]:
        copy.start()
    for c in range(nch):
        pltpu.make_async_copy(left_u.at[:, :, c], ug.at[c, own], load_sem.at[5]).start()

    barrier = pltpu.get_barrier_semaphore()
    for dx in range(1, nx):
        pl.semaphore_signal(barrier, inc=1, device_id={"cols": co_at(dx)}, device_id_type=MESH)
    pl.semaphore_signal(barrier, inc=1, device_id={"cols": partner}, device_id_type=MESH)
    for dy in range(1, ny):
        pl.semaphore_signal(barrier, inc=1, device_id={"inner": y_at(dy)}, device_id_type=MESH)
    for dz in range(1, nz):
        pl.semaphore_signal(barrier, inc=1, device_id={"inner": z_at(dz)}, device_id_type=MESH)
    pl.semaphore_wait(barrier, nx - 1 + 1 + ny - 1 + nz - 1)

    for i in range(tpd):
        for dx in range(1, nx):
            remote(left_v.at[i], vg.at[me_co * tpd + i], V_OUT, v_sem.at[0, i, dx], cols=co_at(dx)).start()
    remote(left_v, vg.at[own], V_OUT, v_sem.at[0, 0, 0], cols=partner).start()
    for c in range(nch):
        for dx in range(1, nx):
            remote(left_u.at[:, :, c], ug.at[c, own], U_OUT, u_sem.at[0, c, dx], cols=co_at(dx)).start()
    for c in range(nch):
        remote(left_u.at[:, :, c], ug.at[c, own], U_OUT, u_sem.at[0, 0, 0], cols=partner).start()

    for copy in tables:
        copy.wait()
    for j in range(n_out):
        named = [lax.rem(index[j, s], tiles) for s in range(slots)]
        alive = [mask[j, s] for s in range(slots)]
        for k in range(tiles):
            at, live = jnp.int32(0), jnp.int32(0)
            for s in range(slots):
                hit = named[s] == k
                at = jnp.where(hit, s, at)
                live = jnp.where(hit, alive[s], live)
            inv[j, k] = at
            lv[j, k] = live

    first_sketch.wait()

    @pl.loop(0, n_out)
    def _(j):
        skt[...] = jnp.transpose(sk[j])
        pltpu.make_async_copy(right_v.at[j], rv.at[j], rv_sem.at[j]).wait()
        for s in range(0, slots, 2):
            out = mm(skt[...], wide([rv[j, s], rv[j, s + 1]]), NN)
            for i in range(2):
                hi, lo = split(out[:, i * rk : (i + 1) * rk])
                pb[j, s + i, :rk] = hi
                pb[j, s + i, rk:] = lo

    own_v.wait()
    ru_load.wait()

    def pair(k):
        vt = jnp.transpose(vg[k])
        for first in range(0, n_out, 2):
            js = (first, first + 1)
            at = [inv[j, k] for j in js]
            out = mm(vt, wide([ru[j, s] for j, s in zip(js, at)]), NN)
            for i, (j, s) in enumerate(zip(js, at)):
                hi, lo = split(out[:, i * rk : (i + 1) * rk] * lv[j, k].astype(F32))
                both = wide([hi, lo])
                pk[j, k] = both
                probe = pb[j, s]
                mixed = mm(both, wide([probe, probe]), NT)
                mix[k, :, j * rk : (j + 1) * rk] = (mixed[:, :rk] + mixed[:, rk:]).astype(BF16)

    def fold_one(k):
        for j in range(n_out):
            right = rv[j, inv[j, k]]
            hi, lo = split(mm(wide([right, right]), pk[j, k], NT))
            wt[j, k, 0] = hi
            wt[j, k, 1] = lo

    folds = []

    def fold(n):
        todo = [folds.pop(0) for _ in range(min(n, len(folds)))]
        for k in todo:
            fold_one(k)

    for i in range(tpd):
        k = me_co * tpd + i
        pair(k)
        folds.append(k)
    arrived(vg.at[pl.ds(partner * tpd, tpd)], v_sem.at[0, 0, 0])
    for i in range(tpd):
        k = partner * tpd + i
        pair(k)
        folds.append(k)

    for i in range(tpd):
        for dx in range(1, nx):
            k = co_at(nx - dx) * tpd + i
            arrived(vg.at[k], v_sem.at[0, i, dx])
            remote(vg.at[k], vg.at[k], V_OUT, v_sem.at[1, i, dx], cols=partner).start()
        for dx in range(1, nx):
            k = co_at(nx - dx) * tpd + i
            pair(k)
            folds.append(k)
        for dx in range(1, nx):
            k = other_at(nx - dx) * tpd + i
            arrived(vg.at[k], v_sem.at[1, i, dx])
        for dx in range(1, nx):
            k = other_at(nx - dx) * tpd + i
            pair(k)
            folds.append(k)
        fold(max(1, 2 // tpd))
    pltpu.make_async_copy(left_v, vg.at[own], load_sem.at[5]).wait()
    arrived(vg.at[own], u_sem.at[0, 0, 0])

    def block_u(c, position):
        return ug.at[c, pl.ds(position * tpd, tpd)]

    def chunk_u(c):
        return wide([ug[c, k].reshape(nb // nch, rk) for k in range(tiles)])

    def sketched(c):
        total = mm(chunk_u(c), mix[...].reshape(tiles * rk, n_out * rk), NN)
        low = total.astype(BF16)
        for j in range(n_out):
            at = slice(j * rk, (j + 1) * rk)
            ybuf[c, :, :, j] = total[:, at].reshape(nz, ny, part_rows, rk)
            part = low[:, at].reshape(nz, ny, part_rows, rk)
            for yy in range(ny):
                sbuf[c, yy, :, j] = part[:, yy]
        for dy in range(1, ny):
            remote(sbuf.at[c, lax.rem(y + dy, ny)], r1.at[c, dy], SUM_Y, sum_sem.at[0, c], inner=y_at(dy)).start()

    def second(c):
        total = ybuf[c, :, y]
        arrived(r1.at[c, pl.ds(1, ny - 1)], sum_sem.at[0, c])
        for dy in range(1, ny):
            total = total + r1[c, dy].astype(F32)
        s2f[c] = total
        s2b[c] = total.astype(BF16)
        for dz in range(1, nz):
            remote(s2b.at[c, lax.rem(z + dz, nz)], r2.at[c, dz], SUM_Z, sum_sem.at[1, c], inner=z_at(dz)).start()

    def last(c):
        total = s2f[c, z]
        arrived(r2.at[c, pl.ds(1, nz - 1)], sum_sem.at[1, c])
        for dz in range(1, nz):
            total = total + r2[c, dz].astype(F32)
        yrow[:, c * part_rows : (c + 1) * part_rows] = total
        yb[c, me_in] = total.astype(BF16)
        part = yb.at[c, me_in]
        for dz in range(1, nz):
            remote(part, part, GATHER, ag_sem.at[c, dz], inner=z_at(dz)).start()
        for dy in range(1, ny):
            remote(part, part, GATHER, ag_sem.at[c, 0], inner=y_at(dy)).start()

    def spread(c):
        for dz in range(1, nz):
            part = yb.at[c, z_at(nz - dz)]
            arrived(part, ag_sem.at[c, dz])
            for dy in range(1, ny):
                remote(part, part, GATHER, ag_sem.at[c, 0], inner=y_at(dy)).start()

    def complete(c):
        arrived(yb.at[c, pl.ds(0, (ny - 1) * nz)], ag_sem.at[c, 0])

    span = nch // groups

    def tile_t(j, g):
        left = wide([wt[j, k, h] for h in range(2) for k in range(tiles)])
        right = jnp.concatenate([chunk_u(g * span + i) for i in range(span)], axis=0)
        for h, part in enumerate(split(mm(left, wide([right, right]), NT))):
            part = part.reshape(nz, ny, rows, nb // groups)
            for yy in range(ny):
                ct[j, g, h, yy] = part[:, yy].reshape(nz * rows, nb // groups)

    def y_of(j):
        return jnp.concatenate([yb[c, :, j].reshape(nb // nch, rk) for c in range(nch)], axis=0)

    def back(j):
        right = y_of(j)
        right = jnp.concatenate([right, right], axis=0)

        def share(yy):
            left = wide([ct[j, g, h, yy] for h in range(2) for g in range(groups)])
            return mm(left, right, NN).reshape(nz, rows, rk)

        for dy in range(1, ny):
            csbuf[j, dy] = share(lax.rem(y + dy, ny)).astype(BF16)
            remote(csbuf.at[j, dy], cr1.at[j, dy], BACK_Y, back_sem.at[0, j], inner=y_at(dy)).start()
        cbuf[j] = share(y)

    def back_second(j):
        total = cbuf[j]
        arrived(cr1.at[j, pl.ds(1, ny - 1)], back_sem.at[0, j])
        for dy in range(1, ny):
            total = total + cr1[j, dy].astype(F32)
        cs2f[j] = total
        cs2b[j] = total.astype(BF16)
        for dz in range(1, nz):
            remote(cs2b.at[j, lax.rem(z + dz, nz)], cr2.at[j, dz], BACK_Z, back_sem.at[1, j], inner=z_at(dz)).start()

    def back_last(j):
        total = cs2f[j, z]
        arrived(cr2.at[j, pl.ds(1, nz - 1)], back_sem.at[1, j])
        for dz in range(1, nz):
            total = total + cr2[j, dz].astype(F32)
        return total

    work = [(j, g) for g in range(groups) for j in range(n_out)]

    def some(n):
        for _ in range(n):
            if work:
                tile_t(*work.pop(0))

    for c in range(nch):
        for dx in range(1, nx):
            part = block_u(c, co_at(nx - dx))
            arrived(part, u_sem.at[0, c, dx])
            remote(part, part, U_OUT, u_sem.at[1, c, dx], cols=partner).start()
        fold(1)
        for dx in range(1, nx):
            arrived(block_u(c, other_at(nx - dx)), u_sem.at[1, c, dx])
        sketched(c)
    fold(len(folds))
    for c in range(nch):
        second(c)
        some(1)
    for c in range(nch):
        last(c)
        some(1)
    some(len(work))
    for c in range(nch):
        spread(c)
    for c in range(nch):
        complete(c)
    for j in range(n_out):
        back(j)

    row_id = lax.broadcasted_iota(jnp.int32, (rk, rk), 0)
    col_id = lax.broadcasted_iota(jnp.int32, (rk, rk), 1)
    for j in range(n_out):
        summed = y_of(j)
        gram = mm(summed, summed, TN)
        diag = jnp.where(row_id == col_id, gram, 0.0)
        s_row = lax.rsqrt(jnp.sum(diag, axis=0, keepdims=True))
        s_col = lax.rsqrt(jnp.sum(diag, axis=1, keepdims=True))
        scale[j] = s_row
        xm[j] = gram * s_col * s_row

    sub8 = lax.broadcasted_iota(jnp.int32, (8, rk), 0)
    lane8 = lax.broadcasted_iota(jnp.int32, (8, rk), 1)

    def eliminate(start, stop):
        @pl.loop(start, stop)
        def _(b):
            base = pl.multiple_of(b * 8, 8)
            near = lane8 - base
            at = pl.ds(base, 8)
            slabs = [xm[j, at] for j in range(n_out)]
            cols = [
                [
                    jnp.broadcast_to(jnp.sum(jnp.where(near == i, slab, 0.0), axis=1, keepdims=True), (8, rk))
                    for i in range(8)
                ]
                for slab in slabs
            ]
            pivots = [jnp.ones((8, rk), F32)] * n_out
            for k in range(8):
                hot = jnp.where(near[:1] == k, 1.0, 0.0)
                for j in range(n_out):
                    column = cols[j][k]
                    pivots[j] = jnp.where(sub8 == k, column[k : k + 1], pivots[j])
                    weight = jnp.where(sub8 > k, column * (1.0 / column[k : k + 1]), 0.0)
                    slabs[j] = slabs[j] - weight * (slabs[j][k : k + 1] + hot)
                    for i in range(k + 1, 8):
                        cols[j][i] = cols[j][i] - weight * cols[j][i][k : k + 1]
            for j in range(n_out):
                ahead = jnp.where(near >= 8, slabs[j] / pivots[j], 0.0)
                unit = jnp.where(near == sub8, 1.0, jnp.where((near >= 0) & (near > sub8) & (near < 8), 0.0, slabs[j]))
                near_all = col_id - base
                clear = (row_id - base >= 8) & (near_all >= 0) & (near_all < 8)
                xm[j] = jnp.where(clear, 0.0, xm[j]) - mm_f32(ahead, unit, TN)
                xm[j, at] = slabs[j]

    blocks = rk // 8
    done = 0
    for j in range(n_out):
        upto = min(blocks, blocks * (5 + 2 * j) // 16)
        eliminate(done, upto)
        done = upto
        back_second(j)
    eliminate(done, blocks)

    for j in range(n_out):
        left = xm[j]
        pivots = jnp.sum(jnp.where(row_id == col_id, left, 0.0), axis=1, keepdims=True)
        lower = jnp.where(col_id < row_id, left, jnp.where(row_id == col_id, 1.0, 0.0))
        inverse = lower * lax.rsqrt(pivots) * scale[j]
        outs[0, j] = mm_f32(yrow[j], inverse, NT)
        outs[1, j] = mm_f32(back_last(j) * 0.5, inverse, NT)

    def gone(ref, kind):
        pltpu.make_async_copy(ref, ref, send_sem.at[kind]).wait()

    gone(vg.at[pl.ds(0, tiles - tpd)], V_OUT)
    gone(vg.at[pl.ds(0, tiles - tpd)], U_OUT)
    gone(r1.at[:, pl.ds(1, ny - 1)], SUM_Y)
    gone(r2.at[:, pl.ds(1, nz - 1)], SUM_Z)
    gone(yb.at[:, pl.ds(0, n_in - 1)], GATHER)
    gone(cr1.at[:, pl.ds(1, ny - 1)], BACK_Y)
    gone(cr2.at[:, pl.ds(1, nz - 1)], BACK_Z)


def body(n_in, n_co, left_u, left_v, right_u, right_v, sketch, tile_index, slot_mask):
    n_out, slots, nb, rk = right_u.shape
    tpd = left_u.shape[0]
    tiles = tpd * n_co
    nx = n_co // 2
    ny = nx
    nz = n_in // ny
    rows = nb // n_in
    nch = rows // 16
    part_rows = rows // nch
    groups = max(1, nch // 2)
    both = pl.pallas_call(
        functools.partial(kernel, n_in, n_co),
        out_shape=jax.ShapeDtypeStruct((2, n_out, rows, rk), F32),
        in_specs=[pl.BlockSpec(memory_space=pl.ANY)] * 7,
        out_specs=pl.BlockSpec(memory_space=pltpu.VMEM),
        scratch_shapes=[
            pltpu.VMEM((nch, tiles, n_in, part_rows, rk), BF16),
            pltpu.VMEM((tiles, nb, rk), BF16),
            pltpu.VMEM((n_out, slots, nb, rk), BF16),
            pltpu.VMEM((n_out, slots, nb, rk), BF16),
            pltpu.VMEM((n_out, nb, rk), BF16),
            pltpu.VMEM((rk, nb), BF16),
            pltpu.SMEM((n_out, slots), jnp.int32),
            pltpu.SMEM((n_out, slots), jnp.int32),
            pltpu.SMEM((n_out, tiles), jnp.int32),
            pltpu.SMEM((n_out, tiles), jnp.int32),
            pltpu.VMEM((n_out, slots, 2 * rk, rk), BF16),
            pltpu.VMEM((n_out, tiles, rk, 2 * rk), BF16),
            pltpu.VMEM((tiles, rk, n_out * rk), BF16),
            pltpu.VMEM((n_out, tiles, 2, nb, rk), BF16),
            pltpu.VMEM((n_out, groups, 2, ny, nz * rows, nb // groups), BF16),
            pltpu.VMEM((nch, nz, ny, n_out, part_rows, rk), F32),
            pltpu.VMEM((nch, ny, nz, n_out, part_rows, rk), BF16),
            pltpu.VMEM((nch, ny, nz, n_out, part_rows, rk), BF16),
            pltpu.VMEM((nch, nz, n_out, part_rows, rk), F32),
            pltpu.VMEM((nch, nz, n_out, part_rows, rk), BF16),
            pltpu.VMEM((nch, nz, n_out, part_rows, rk), BF16),
            pltpu.VMEM((n_out, rows, rk), F32),
            pltpu.VMEM((nch, n_in, n_out, part_rows, rk), BF16),
            pltpu.VMEM((n_out, nz, rows, rk), F32),
            pltpu.VMEM((n_out, ny, nz, rows, rk), BF16),
            pltpu.VMEM((n_out, ny, nz, rows, rk), BF16),
            pltpu.VMEM((n_out, nz, rows, rk), F32),
            pltpu.VMEM((n_out, nz, rows, rk), BF16),
            pltpu.VMEM((n_out, nz, rows, rk), BF16),
            pltpu.VMEM((n_out, rk, rk), F32),
            pltpu.VMEM((n_out, 1, rk), F32),
            pltpu.SemaphoreType.DMA((6,)),
            pltpu.SemaphoreType.DMA((n_out,)),
            pltpu.SemaphoreType.DMA((7,)),
            pltpu.SemaphoreType.DMA((2, tpd, nx)),
            pltpu.SemaphoreType.DMA((2, nch, nx)),
            pltpu.SemaphoreType.DMA((2, nch)),
            pltpu.SemaphoreType.DMA((nch, nz)),
            pltpu.SemaphoreType.DMA((2, n_out)),
        ],
        compiler_params=pltpu.CompilerParams(
            collective_id=0, has_side_effects=True, vmem_limit_bytes=60 * 1024 * 1024
        ),
    )(left_u.reshape(tpd, n_in, nch, part_rows, rk), left_v, right_u, right_v, sketch, tile_index, slot_mask)
    return both[0] * math.sqrt(nb), both[1] * 2.0


def solution(mesh):
    return jax.shard_map(
        functools.partial(body, mesh.shape["inner"], mesh.shape["cols"]),
        mesh=mesh,
        in_specs=(
            P(("inner", "cols"), None, None),
            P(("inner", "cols"), None, None),
            P("cols", "inner", None, None),
            P("cols", "inner", None, None),
            P("cols", None, None),
            P("cols", "inner"),
            P("cols", "inner"),
        ),
        out_specs=(P("cols", "inner", None), P("cols", "inner", None)),
        check_vma=False,
    )
```

time: 61.6 us -> 57.2 us (0.929)
  local copies, waits for them, and re-layouts: 3.14 us -> 0 us
  Pallas kernels: 57.7 us -> 54.7 us
  other arithmetic: 0 us -> 1.69 us
    unnamed x2 -> x0, local copies, waits for them, and re-layouts: 3.14 us -> none
    pallas_call x1, Pallas kernels: 57.7 us -> 54.7 us  [body(): pl.pallas_call(functools.partial(kernel, n_in, n_co), out_shape=jax.Shape...]
    mul x0 -> x1, other arithmetic: none -> 1.69 us  [body(): return (both[0] * math.sqrt(nb), both[1] * 2.0)]
where the time goes in v2:
time: 57.2 us; the launch traced here: 57.1 us
  Pallas kernels  54.7 us (96%)
  other arithmetic  1.69 us (3%)
  between operations  0.64 us (1%)
    pallas_call x1, Pallas kernels, body(): pl.pallas_call(functools.partial(kernel, n_in, n_co), out_shape=jax.Shape...  54.7 us
    mul x1, other arithmetic, body(): return (both[0] * math.sqrt(nb), both[1] * 2.0)  1.69 us

profile of v2, /device:TPU:0, one launch (start us, length us, event | category | flops | bytes accessed | tf_op | source)
XLA Modules:
  0.0 57.1 jit_solution(3798745438907898707)
XLA Ops:
  0.6 54.7 %shard_map.86 = f32[2,4,64,128]{3,2,1,0:T(8,128)} custom-call(bf16[2,8,4,16,128]{4,3,2,1,0:T(8,128)(2,1)} %bitcast.5, bf16[2,512,128]{2,1,0:T(8,128)(2,1)} %left_v.1, bf16[4,8,512,128]{3,2,1,0:T(8,128)(2,1)} %right_u.1, bf16[4,8,512,128]{3,2,1,0:T(8,128)(2,1)} %right_v.1, bf16[4,512,128]{2,1,0:T(8,128)(2,1)} %sketch.1, s32[4,8]{1,0:T(4,128)} %index_hbm.1, ...), custom_call_target="tpu_custom_call" | custom-call | tf_op jit(solution)/shard_map/pallas_call | solution.py:411
  55.4 1.7 %multiply_bitcast_fusion = (f32[4,64,128]{2,1,0:T(8,128)}, f32[4,64,128]{2,1,0:T(8,128)}) fusion(f32[2,4,64,128]{3,2,1,0:T(8,128)} %shard_map.86), kind=kLoop, calls=%fused_computation | loop fusion | flops 65536 | bytes 524288 | tf_op jit(solution)/shard_map/mul | solution.py:461

commit v3 on v2

v3 whole, which is shorter than its diff:
```python
import functools
import math

import jax
import jax.numpy as jnp
from jax import lax
from jax.experimental import pallas as pl
from jax.experimental.pallas import tpu as pltpu
from jax.sharding import PartitionSpec as P

MESH = pl.DeviceIdType.MESH
F32 = jnp.float32
BF16 = jnp.bfloat16
NN = (((1,), (0,)), ((), ()))
NT = (((1,), (1,)), ((), ()))
TN = (((0,), (0,)), ((), ()))


def mm(a, b, dims):
    return lax.dot_general(a, b, dims, preferred_element_type=F32)


def split(a):
    hi = a.astype(BF16)
    return hi, (a - hi.astype(F32)).astype(BF16)


LEFT = (0, 0, 1, 1, 0, 2)
RIGHT = (0, 1, 0, 1, 2, 0)


def stack(a, order):
    first = a.astype(BF16).astype(F32)
    second = (a - first).astype(BF16).astype(F32)
    parts = (first, second, a - first - second)
    return jnp.concatenate([parts[i] for i in order], axis=0).astype(BF16)


def wide(parts):
    return jnp.concatenate(parts, axis=1)


def kernel(
    n_in, n_co, left_u, left_v, right_u, right_v, sketch, index_hbm, mask_hbm, outs,
    ug, vg, ru, rv, sk, skt, index, mask, inv, lv, pb, pk, mix, wt, ct,
    ybuf, sbuf, r1, s2f, s2b, r2, r3, yrow, yb,
    cbuf, csbuf, cr1, cs2f, cs2b, cr2, xm, scale, inverse,
    load_sem, rv_sem, send_sem, v_sem, u_sem, sum_sem, ag_sem, back_sem,
):
    nx = n_co // 2
    ny = nx
    nz = n_in // ny
    tpd, nb, rk = left_v.shape
    nch, part_rows = ug.shape[0], ug.shape[3]
    groups = ct.shape[1]
    cuts = cbuf.shape[1]
    tiles = tpd * n_co
    n_out, slots = right_u.shape[:2]
    rows = nb // n_in
    me_in = lax.axis_index("inner")
    me_co = lax.axis_index("cols")
    x, core = lax.div(me_co, 2), lax.rem(me_co, 2)
    z, y = lax.div(me_in, ny), lax.rem(me_in, ny)
    def co_at(dx):
        return lax.rem(x + dx, nx) * 2 + core

    def other_at(dx):
        return lax.rem(x + dx, nx) * 2 + (1 - core)

    partner = other_at(0)

    def z_at(dz):
        return lax.rem(z + dz, nz) * ny + y

    def y_at(dy):
        return z * ny + lax.rem(y + dy, ny)

    half = nz // 2
    depth = jnp.minimum(z, nz - 1 - z)
    inwards = jnp.where(z < half, 1, -1)
    inner_at = (z + inwards) * ny + y
    outer_at = (z - inwards) * ny + y

    parts = []
    for c in range(nch):
        n = n_out // 2 if c < nch - 1 else 1
        parts += [(c, j, n) for j in range(0, n_out, n)]
    V_OUT, U_OUT, SUM_Y, SUM_Z, GATHER_Z, GATHER_Y, BACK_Y, BACK_Z = range(8)

    def remote(src, dst, kind, r_sem, **dev):
        return pltpu.make_async_remote_copy(
            src_ref=src, dst_ref=dst, send_sem=send_sem.at[kind], recv_sem=r_sem,
            device_id=dev, device_id_type=MESH,
        )

    def arrived(part, r_sem):
        pltpu.make_async_copy(part, part, r_sem).wait()

    own = pl.ds(me_co * tpd, tpd)
    tables = [pltpu.make_async_copy(index_hbm, index, load_sem.at[0]), pltpu.make_async_copy(mask_hbm, mask, load_sem.at[1])]
    first_sketch = pltpu.make_async_copy(sketch, sk, load_sem.at[2])
    rv_load = [pltpu.make_async_copy(right_v.at[j], rv.at[j], rv_sem.at[j]) for j in range(n_out)]
    own_v = pltpu.make_async_copy(left_v, vg.at[own], load_sem.at[3])
    ru_load = pltpu.make_async_copy(right_u, ru, load_sem.at[4])
    for copy in tables + [first_sketch] + rv_load[:2]:
        copy.start()

    barrier = pltpu.get_barrier_semaphore()
    for dx in range(1, nx):
        pl.semaphore_signal(barrier, inc=1, device_id={"cols": co_at(dx)}, device_id_type=MESH)
    pl.semaphore_signal(barrier, inc=1, device_id={"cols": partner}, device_id_type=MESH)
    for dy in range(1, ny):
        pl.semaphore_signal(barrier, inc=1, device_id={"inner": y_at(dy)}, device_id_type=MESH)
    for dz in range(1, nz):
        pl.semaphore_signal(barrier, inc=1, device_id={"inner": z_at(dz)}, device_id_type=MESH)
    pl.semaphore_wait(barrier, nx - 1 + 1 + ny - 1 + nz - 1)

    for i in range(tpd):
        for dx in range(1, nx):
            remote(left_v.at[i], vg.at[me_co * tpd + i], V_OUT, v_sem.at[1 + 2 * ((dx - 1) * tpd + i)], cols=co_at(dx)).start()
    for c in range(nch):
        for dx in range(1, nx):
            remote(left_u.at[:, :, c], ug.at[c, own], U_OUT, u_sem.at[1 + 2 * ((dx - 1) * nch + c)], cols=co_at(dx)).start()
    for copy in rv_load[2:] + [own_v]:
        copy.start()
    remote(left_v, vg.at[own], V_OUT, v_sem.at[0], cols=partner).start()
    ru_load.start()
    for c in range(nch):
        pltpu.make_async_copy(left_u.at[:, :, c], ug.at[c, own], load_sem.at[5]).start()
    for c in range(nch):
        remote(left_u.at[:, :, c], ug.at[c, own], U_OUT, u_sem.at[0], cols=partner).start()

    for copy in tables:
        copy.wait()
    for j in range(n_out):
        named = [lax.rem(index[j, s], tiles) for s in range(slots)]
        alive = [mask[j, s] for s in range(slots)]
        for k in range(tiles):
            at, live = jnp.int32(0), jnp.int32(0)
            for s in range(slots):
                hit = named[s] == k
                at = jnp.where(hit, s, at)
                live = jnp.where(hit, alive[s], live)
            inv[j, k] = at
            lv[j, k] = live

    first_sketch.wait()

    @pl.loop(0, n_out)
    def _(j):
        skt[...] = jnp.transpose(sk[j])
        pltpu.make_async_copy(right_v.at[j], rv.at[j], rv_sem.at[j]).wait()
        for s in range(0, slots, 2):
            out = mm(skt[...], wide([rv[j, s], rv[j, s + 1]]), NN)
            for i in range(2):
                hi, lo = split(out[:, i * rk : (i + 1) * rk])
                pb[j, s + i, :rk] = hi
                pb[j, s + i, rk:] = lo

    own_v.wait()
    ru_load.wait()

    def pair(k):
        vt = jnp.transpose(vg[k])
        for first in range(0, n_out, 2):
            js = (first, first + 1)
            at = [inv[j, k] for j in js]
            out = mm(vt, wide([ru[j, s] for j, s in zip(js, at)]), NN)
            for i, (j, s) in enumerate(zip(js, at)):
                hi, lo = split(out[:, i * rk : (i + 1) * rk] * lv[j, k].astype(F32))
                both = wide([hi, lo])
                pk[j, k] = both
                probe = pb[j, s]
                mixed = mm(both, wide([probe, probe]), NT)
                mix[k, :, j * rk : (j + 1) * rk] = (mixed[:, :rk] + mixed[:, rk:]).astype(BF16)

    def fold_one(k):
        for j in range(n_out):
            right = rv[j, inv[j, k]]
            wt[j, k, 0], wt[j, k, 1] = split(mm(wide([right, right]), pk[j, k], NT))

    folds = []

    def fold(n):
        todo = [folds.pop(0) for _ in range(min(n, len(folds)))]
        for k in todo:
            fold_one(k)

    for i in range(tpd):
        k = me_co * tpd + i
        pair(k)
        folds.append(k)
    arrived(vg.at[pl.ds(partner * tpd, tpd)], v_sem.at[0])
    for i in range(tpd):
        k = partner * tpd + i
        pair(k)
        folds.append(k)

    for i in range(tpd):
        for dx in range(1, nx):
            k = co_at(nx - dx) * tpd + i
            arrived(vg.at[k], v_sem.at[1 + 2 * ((dx - 1) * tpd + i)])
            remote(vg.at[k], vg.at[k], V_OUT, v_sem.at[2 + 2 * ((dx - 1) * tpd + i)], cols=partner).start()
        for dx in range(1, nx):
            k = co_at(nx - dx) * tpd + i
            pair(k)
            folds.append(k)
        fold(1)
        for dx in range(1, nx):
            k = other_at(nx - dx) * tpd + i
            arrived(vg.at[k], v_sem.at[2 + 2 * ((dx - 1) * tpd + i)])
        for dx in range(1, nx):
            k = other_at(nx - dx) * tpd + i
            pair(k)
            folds.append(k)
        if i < tpd - 1:
            fold(1)
    pltpu.make_async_copy(left_v, vg.at[own], load_sem.at[5]).wait()
    arrived(vg.at[own], u_sem.at[0])

    def block_u(c, position):
        return ug.at[c, pl.ds(position * tpd, tpd)]

    def chunk_u(c):
        return wide([ug[c, k].reshape(nb // nch, rk) for k in range(tiles)])

    def sketched(c):
        total = mm(chunk_u(c), mix[...].reshape(tiles * rk, n_out * rk), NN)
        low = total.astype(BF16)
        for j in range(n_out):
            at = slice(j * rk, (j + 1) * rk)
            shape = (nz, ny, part_rows, rk)
            full = total[:, at].reshape(shape)
            part = low[:, at].reshape(shape)
            for yy in range(ny):
                ybuf[c, yy, :, j] = full[:, yy]
                sbuf[c, yy, :, j] = part[:, yy]
        for q, (of, first, n) in enumerate(parts):
            if of == c:
                at = pl.ds(first, n)
                for dy in range(1, ny):
                    remote(
                        sbuf.at[c, lax.rem(y + dy, ny), :, at], r1.at[c, dy, :, at],
                        SUM_Y, sum_sem.at[0, q], inner=y_at(dy),
                    ).start()

    def second(q):
        c, first, n = parts[q]
        at = pl.ds(first, n)
        arrived(r1.at[c, pl.ds(1, ny - 1), :, at], sum_sem.at[0, q])
        total = ybuf[c, y, :, at]
        for dy in range(1, ny):
            total = total + r1[c, dy, :, at].astype(F32)
        s2f[c, :, at] = total
        if half > 1:
            @pl.when(depth == 0)
            def _():
                s2b[c, :, at] = total.astype(BF16)
                remote(s2b.at[c, :, at], r2.at[c, :, at], SUM_Z, sum_sem.at[1, q], inner=inner_at).start()

    def third(q, level):
        c, first, n = parts[q]
        at = pl.ds(first, n)

        @pl.when(depth == level)
        def _():
            arrived(r2.at[c, :, at], sum_sem.at[1, q])
            total = s2f[c, :, at] + r2[c, :, at].astype(F32)
            s2b[c, :, at] = total.astype(BF16)
            land, sem = (r2, 1) if level < half - 1 else (r3, 2)
            remote(s2b.at[c, :, at], land.at[c, :, at], SUM_Z, sum_sem.at[sem, q], inner=inner_at).start()
            s2f[c, :, at] = total

    def to_y(q):
        c, first, n = parts[q]
        part = yb.at[c, y, :, pl.ds(first, n)]
        for dy in range(1, ny):
            remote(part, part, GATHER_Y, ag_sem.at[q], inner=y_at(dy)).start()

    def to_outer(q):
        c, first, n = parts[q]
        part = yb.at[c, y, :, pl.ds(first, n)]
        remote(part, part, GATHER_Z, sum_sem.at[1, q], inner=outer_at).start()

    def last(q):
        c, first, n = parts[q]
        at = pl.ds(first, n)

        @pl.when(depth == half - 1)
        def _():
            arrived(r3.at[c, :, at], sum_sem.at[2, q])
            total = s2f[c, :, at] + r3[c, :, at].astype(F32)
            yb[c, y, :, at] = total.astype(BF16)
            if half > 1:
                to_outer(q)
            to_y(q)
            s2f[c, :, at] = total
            yrow[at, c * part_rows : (c + 1) * part_rows] = s2f[c, z, at]

    def spread(q, level):
        c, first, n = parts[q]
        at = pl.ds(first, n)

        @pl.when(depth == level)
        def _():
            arrived(yb.at[c, y, :, at], sum_sem.at[1, q])
            if level > 0:
                to_outer(q)
            to_y(q)
            yrow[at, c * part_rows : (c + 1) * part_rows] = yb[c, y, z, at].astype(F32)

    def complete(q):
        c, first, n = parts[q]
        arrived(yb.at[c, pl.ds(0, ny - 1), :, pl.ds(first, n)], ag_sem.at[q])

    span = nch // groups

    def tile_t(j, g):
        left = wide([wt[j, k, h] for h in range(2) for k in range(tiles)])
        right = jnp.concatenate([chunk_u(g * span + i) for i in range(span)], axis=0)
        for h, part in enumerate(split(mm(left, wide([right, right]), NT))):
            part = part.reshape(nz, ny, rows, nb // groups)
            for yy in range(ny):
                ct[j, g, h, yy] = part[:, yy].reshape(nz * rows, nb // groups)

    def y_chunk(c, j):
        return jnp.concatenate([yb[c, yy, zz, j] for zz in range(nz) for yy in range(ny)], axis=0)

    def y_of(j):
        return jnp.concatenate([y_chunk(c, j) for c in range(nch)], axis=0)

    def back(j):
        right = y_of(j)
        right = jnp.concatenate([right, right], axis=0)

        def share(yy):
            left = wide([ct[j, g, h, yy] for h in range(2) for g in range(groups)])
            return mm(left, right, NN).reshape(nz, cuts, rows // cuts, rk)

        for dy in range(1, ny):
            part = share(lax.rem(y + dy, ny)).astype(BF16)
            for p in range(cuts):
                csbuf[j, p, dy] = part[:, p]
                remote(
                    csbuf.at[j, p, dy], cr1.at[j, p, dy], BACK_Y, back_sem.at[0, j, p], inner=y_at(dy)
                ).start()
        part = share(y)
        for p in range(cuts):
            cbuf[j, p] = part[:, p]

    def back_second(j, p):
        total = cbuf[j, p]
        arrived(cr1.at[j, p, pl.ds(1, ny - 1)], back_sem.at[0, j, p])
        for dy in range(1, ny):
            total = total + cr1[j, p, dy].astype(F32)
        cs2f[j, p] = total
        cs2b[j, p] = total.astype(BF16)
        for dz in range(1, nz):
            remote(
                cs2b.at[j, p, lax.rem(z + dz, nz)], cr2.at[j, p, dz], BACK_Z, back_sem.at[1, j, p], inner=z_at(dz)
            ).start()

    def back_last(j):
        parts = []
        for p in range(cuts):
            total = cs2f[j, p, z]
            arrived(cr2.at[j, p, pl.ds(1, nz - 1)], back_sem.at[1, j, p])
            for dz in range(1, nz):
                total = total + cr2[j, p, dz].astype(F32)
            parts.append(total)
        return jnp.concatenate(parts, axis=0)

    work = [(j, g) for g in range(groups) for j in range(n_out)]

    def pass_on_u(c):
        for dx in range(1, nx):
            part = block_u(c, co_at(nx - dx))
            arrived(part, u_sem.at[1 + 2 * ((dx - 1) * nch + c)])
            remote(part, part, U_OUT, u_sem.at[2 + 2 * ((dx - 1) * nch + c)], cols=partner).start()

    def gram(c):
        for j in range(n_out):
            part = y_chunk(c, j)
            total = mm(part, part, TN)
            xm[j] = total if c == 0 else xm[j] + total

    pass_on_u(0)
    for c in range(nch):
        if c == 0:
            fold(1)
        if c < nch - 1:
            pass_on_u(c + 1)
        if c == nch - 1:
            fold(2)
        for dx in range(1, nx):
            arrived(block_u(c, other_at(nx - dx)), u_sem.at[2 + 2 * ((dx - 1) * nch + c)])
        sketched(c)
        if c == 1:
            fold(1)

    count = len(parts)
    stages = [second]
    stages += [functools.partial(third, level=i) for i in range(1, half)]
    stages += [last]
    stages += [functools.partial(spread, level=i) for i in range(half - 2, -1, -1)]
    times = {}
    for q, (c, first, n) in enumerate(parts):
        start = 1.4 * (c + 0.7 * first / n_out)
        for i in range(len(stages)):
            times[i, q] = start + (0.0, *[3.1 + 3.6 * h for h in range(half)], *[2.4 * (h + 1) + 3.6 * half - 0.5 for h in range(half - 1)])[i]
    order = sorted(times, key=times.get)
    def products(here):
        @pl.when(here)
        def _():
            for j, g in work:
                tile_t(j, g)

    for i, q in order:
        stages[i](q)
        if (i, q) == (0, 1):
            fold(len(folds))
        if (i, q) == (0, count - 1):
            products(depth < half - 1)
        if (i, q) == (half, count - 1):
            products(depth == half - 1)
    for c in range(nch):
        for q in range(count):
            if parts[q][0] == c:
                complete(q)
                if c == nch - 1:
                    back(parts[q][1])
        if c < nch - 1:
            gram(c)
    gram(nch - 1)
    row_id = lax.broadcasted_iota(jnp.int32, (rk, rk), 0)
    col_id = lax.broadcasted_iota(jnp.int32, (rk, rk), 1)
    for j in range(n_out):
        whole = xm[j]
        diag = jnp.where(row_id == col_id, whole, 0.0)
        s_row = lax.rsqrt(jnp.sum(diag, axis=0, keepdims=True))
        s_col = lax.rsqrt(jnp.sum(diag, axis=1, keepdims=True))
        scale[j] = s_row
        xm[j] = whole * s_col * s_row

    sub8 = lax.broadcasted_iota(jnp.int32, (8, rk), 0)
    lane8 = lax.broadcasted_iota(jnp.int32, (8, rk), 1)

    def eliminate(start, stop):
        @pl.loop(start, stop)
        def _(b):
            eliminate_block(b)

    def eliminate_block(b):
        base = b * 8 if isinstance(b, int) else pl.multiple_of(b * 8, 8)
        near = lane8 - base
        at = pl.ds(base, 8)
        slabs = [xm[j, at] for j in range(n_out)]
        cols = [
            [
                jnp.broadcast_to(jnp.sum(jnp.where(near == i, slab, 0.0), axis=1, keepdims=True), (8, rk))
                for i in range(8)
            ]
            for slab in slabs
        ]
        pivots = [jnp.ones((8, rk), F32)] * n_out
        for k in range(8):
            hot = jnp.where(near[:1] == k, 1.0, 0.0)
            for j in range(n_out):
                column = cols[j][k]
                pivots[j] = jnp.where(sub8 == k, column[k : k + 1], pivots[j])
                weight = jnp.where(sub8 > k, column * (1.0 / column[k : k + 1]), 0.0)
                slabs[j] = slabs[j] - weight * (slabs[j][k : k + 1] + hot)
                for i in range(k + 1, 8):
                    cols[j][i] = cols[j][i] - weight * cols[j][i][k : k + 1]
        for j in range(n_out):
            ahead = jnp.where(near >= 8, slabs[j] / pivots[j], 0.0)
            unit = jnp.where(near == sub8, 1.0, jnp.where((near >= 0) & (near > sub8) & (near < 8), 0.0, slabs[j]))
            near_all = col_id - base
            clear = (row_id - base >= 8) & (near_all >= 0) & (near_all < 8)
            xm[j] = jnp.where(clear, 0.0, xm[j]) - mm(stack(ahead, LEFT), stack(unit, RIGHT), TN)
            xm[j, at] = slabs[j]

    blocks = rk // 8
    pieces = [(j, p) for j in range(n_out) for p in range(cuts)]
    done = 0
    for n, (j, p) in enumerate(pieces):
        upto = blocks * (2 * len(pieces) + 10 * n) // (16 * len(pieces))
        if upto > done:
            eliminate(done, upto)
            done = upto
        back_second(j, p)
    eliminate(done, blocks)

    for j in range(n_out):
        left = xm[j]
        pivots = jnp.sum(jnp.where(row_id == col_id, left, 0.0), axis=1, keepdims=True)
        lower = jnp.where(col_id < row_id, left, jnp.where(row_id == col_id, 1.0, 0.0))
        hi, lo = split(lower * lax.rsqrt(pivots) * scale[j])
        inverse[j] = wide([hi, lo, hi])
        hi, lo = split(yrow[j])
        outs[0, j] = mm(wide([hi, hi, lo]), inverse[j], NT)
    for j in range(n_out):
        hi, lo = split(back_last(j) * 0.5)
        outs[1, j] = mm(wide([hi, hi, lo]), inverse[j], NT)

    def gone(ref, kind):
        pltpu.make_async_copy(ref, ref, send_sem.at[kind]).wait()

    gone(vg.at[pl.ds(0, tiles - tpd)], V_OUT)
    gone(vg.at[pl.ds(0, tiles - tpd)], U_OUT)
    gone(r1.at[:, pl.ds(1, ny - 1)], SUM_Y)
    gone(s2b, SUM_Z)
    if half > 1:
        @pl.when(depth > 0)
        def _():
            gone(yb.at[:, 0], GATHER_Z)
    gone(yb.at[:, pl.ds(0, ny - 1)], GATHER_Y)
    gone(cr1.at[:, :, pl.ds(1, ny - 1)], BACK_Y)
    gone(cr2.at[:, :, pl.ds(1, nz - 1)], BACK_Z)


def body(n_in, n_co, left_u, left_v, right_u, right_v, sketch, tile_index, slot_mask):
    n_out, slots, nb, rk = right_u.shape
    tpd = left_u.shape[0]
    tiles = tpd * n_co
    nx = n_co // 2
    ny = nx
    nz = n_in // ny
    rows = nb // n_in
    nch = rows // 16
    part_rows = rows // nch
    groups = max(1, nch // 2)
    count = 2 * (nch - 1) + n_out
    cuts = 2 if rows % 32 == 0 else 1
    both = pl.pallas_call(
        functools.partial(kernel, n_in, n_co),
        out_shape=jax.ShapeDtypeStruct((2, n_out, rows, rk), F32),
        in_specs=[pl.BlockSpec(memory_space=pl.ANY)] * 7,
        out_specs=pl.BlockSpec(memory_space=pltpu.VMEM),
        scratch_shapes=[
            pltpu.VMEM((nch, tiles, n_in, part_rows, rk), BF16),
            pltpu.VMEM((tiles, nb, rk), BF16),
            pltpu.VMEM((n_out, slots, nb, rk), BF16),
            pltpu.VMEM((n_out, slots, nb, rk), BF16),
            pltpu.VMEM((n_out, nb, rk), BF16),
            pltpu.VMEM((rk, nb), BF16),
            pltpu.SMEM((n_out, slots), jnp.int32),
            pltpu.SMEM((n_out, slots), jnp.int32),
            pltpu.SMEM((n_out, tiles), jnp.int32),
            pltpu.SMEM((n_out, tiles), jnp.int32),
            pltpu.VMEM((n_out, slots, 2 * rk, rk), BF16),
            pltpu.VMEM((n_out, tiles, rk, 2 * rk), BF16),
            pltpu.VMEM((tiles, rk, n_out * rk), BF16),
            pltpu.VMEM((n_out, tiles, 2, nb, rk), BF16),
            pltpu.VMEM((n_out, groups, 2, ny, nz * rows, nb // groups), BF16),
            pltpu.VMEM((nch, ny, nz, n_out, part_rows, rk), F32),
            pltpu.VMEM((nch, ny, nz, n_out, part_rows, rk), BF16),
            pltpu.VMEM((nch, ny, nz, n_out, part_rows, rk), BF16),
            pltpu.VMEM((nch, nz, n_out, part_rows, rk), F32),
            pltpu.VMEM((nch, nz, n_out, part_rows, rk), BF16),
            pltpu.VMEM((nch, nz, n_out, part_rows, rk), BF16),
            pltpu.VMEM((nch, nz, n_out, part_rows, rk), BF16),
            pltpu.VMEM((n_out, rows, rk), F32),
            pltpu.VMEM((nch, ny, nz, n_out, part_rows, rk), BF16),
            pltpu.VMEM((n_out, cuts, nz, rows // cuts, rk), F32),
            pltpu.VMEM((n_out, cuts, ny, nz, rows // cuts, rk), BF16),
            pltpu.VMEM((n_out, cuts, ny, nz, rows // cuts, rk), BF16),
            pltpu.VMEM((n_out, cuts, nz, rows // cuts, rk), F32),
            pltpu.VMEM((n_out, cuts, nz, rows // cuts, rk), BF16),
            pltpu.VMEM((n_out, cuts, nz, rows // cuts, rk), BF16),
            pltpu.VMEM((n_out, rk, rk), F32),
            pltpu.VMEM((n_out, 1, rk), F32),
            pltpu.VMEM((n_out, rk, 3 * rk), BF16),
            pltpu.SemaphoreType.DMA((6,)),
            pltpu.SemaphoreType.DMA((n_out,)),
            pltpu.SemaphoreType.DMA((8,)),
            pltpu.SemaphoreType.DMA((1 + 2 * tpd * (nx - 1),)),
            pltpu.SemaphoreType.DMA((1 + 2 * nch * (nx - 1),)),
            pltpu.SemaphoreType.DMA((3, count)),
            pltpu.SemaphoreType.DMA((count,)),
            pltpu.SemaphoreType.DMA((2, n_out, cuts)),
        ],
        compiler_params=pltpu.CompilerParams(
            collective_id=0, has_side_effects=True, vmem_limit_bytes=60 * 1024 * 1024
        ),
    )(left_u.reshape(tpd, n_in, nch, part_rows, rk), left_v, right_u, right_v, sketch, tile_index, slot_mask)
    return both[0] * math.sqrt(nb), both[1] * 2.0


def solution(mesh):
    return jax.shard_map(
        functools.partial(body, mesh.shape["inner"], mesh.shape["cols"]),
        mesh=mesh,
        in_specs=(
            P(("inner", "cols"), None, None),
            P(("inner", "cols"), None, None),
            P("cols", "inner", None, None),
            P("cols", "inner", None, None),
            P("cols", None, None),
            P("cols", "inner"),
            P("cols", "inner"),
        ),
        out_specs=(P("cols", "inner", None), P("cols", "inner", None)),
        check_vma=False,
    )
```

time: 57.2 us -> 51.3 us (0.90)
  Pallas kernels: 54.7 us -> 48.8 us
    pallas_call x1, Pallas kernels: 54.7 us -> 48.8 us  [body(): pl.pallas_call(functools.partial(kernel, n_in, n_co), out_shape=jax.Shape...]
where the time goes in v3:
time: 51.3 us; the launch traced here: 51.1 us
  Pallas kernels  48.8 us (95%)
  other arithmetic  1.69 us (3%)
  between operations  0.64 us (1%)
    pallas_call x1, Pallas kernels, body(): pl.pallas_call(functools.partial(kernel, n_in, n_co), out_shape=jax.Shape...  48.8 us
    mul x1, other arithmetic, body(): return (both[0] * math.sqrt(nb), both[1] * 2.0)  1.69 us

profile of v3, /device:TPU:0, one launch (start us, length us, event | category | flops | bytes accessed | tf_op | source)
XLA Modules:
  0.0 51.1 jit_solution(11654823927396376458)
XLA Ops:
  0.6 48.8 %shard_map.86 = f32[2,4,64,128]{3,2,1,0:T(8,128)} custom-call(bf16[2,8,4,16,128]{4,3,2,1,0:T(8,128)(2,1)} %bitcast.5, bf16[2,512,128]{2,1,0:T(8,128)(2,1)} %left_v.1, bf16[4,8,512,128]{3,2,1,0:T(8,128)(2,1)} %right_u.1, bf16[4,8,512,128]{3,2,1,0:T(8,128)(2,1)} %right_v.1, bf16[4,512,128]{2,1,0:T(8,128)(2,1)} %sketch.1, s32[4,8]{1,0:T(4,128)} %index_hbm.1, ...), custom_call_target="tpu_custom_call" | custom-call | tf_op jit(solution)/shard_map/pallas_call | solution.py:535
  49.4 1.7 %multiply_bitcast_fusion = (f32[4,64,128]{2,1,0:T(8,128)}, f32[4,64,128]{2,1,0:T(8,128)}) fusion(f32[2,4,64,128]{3,2,1,0:T(8,128)} %shard_map.86), kind=kLoop, calls=%fused_computation | loop fusion | flops 65536 | bytes 524288 | tf_op jit(solution)/shard_map/mul | solution.py:587

commit v4 on v3

--- a/solution.py
+++ b/solution.py
@@ -581,9 +581,14 @@
             pltpu.SemaphoreType.DMA((2, n_out, cuts)),
         ],
         compiler_params=pltpu.CompilerParams(
-            collective_id=0, has_side_effects=True, vmem_limit_bytes=60 * 1024 * 1024
+            collective_id=0, has_side_effects=True, vmem_limit_bytes=52 * 1024 * 1024
         ),
-    )(left_u.reshape(tpd, n_in, nch, part_rows, rk), left_v, right_u, right_v, sketch, tile_index, slot_mask)
+    )(*[
+        pltpu.with_memory_space_constraint(a, pltpu.HBM)
+        for a in (
+            left_u.reshape(tpd, n_in, nch, part_rows, rk), left_v, right_u, right_v, sketch, tile_index, slot_mask
+        )
+    ])
     return both[0] * math.sqrt(nb), both[1] * 2.0
 
 

time: 51.3 us -> 49.6 us (0.967)
  other arithmetic: 1.69 us -> 0.72 us
  Pallas kernels: 48.8 us -> 48.1 us
    mul x1, other arithmetic: 1.69 us -> 0.72 us  [body(): return (both[0] * math.sqrt(nb), both[1] * 2.0)]
    pallas_call x1, Pallas kernels: 48.8 us -> 48.1 us  [body(): pl.pallas_call(functools.partial(kernel, n_in, n_co), out_shape=jax.Shape...]
where the time goes in v4:
time: 49.6 us; the launch traced here: 49.5 us
  Pallas kernels  48.1 us (97%)
  other arithmetic  0.72 us (1%)
  between operations  0.64 us (1%)
    pallas_call x1, Pallas kernels, body(): pl.pallas_call(functools.partial(kernel, n_in, n_co), out_shape=jax.Shape...  48.1 us

profile of v4, /device:TPU:0, one launch (start us, length us, event | category | flops | bytes accessed | tf_op | source)
XLA Modules:
  0.0 49.5 jit_solution(6341471038233883988)
XLA Ops:
  0.6 48.1 %shard_map.86 = f32[2,4,64,128]{3,2,1,0:T(8,128)S(1)} custom-call(bf16[2,8,4,16,128]{4,3,2,1,0:T(8,128)(2,1)} %bitcast.5, bf16[2,512,128]{2,1,0:T(8,128)(2,1)} %left_v.1, bf16[4,8,512,128]{3,2,1,0:T(8,128)(2,1)} %right_u.1, bf16[4,8,512,128]{3,2,1,0:T(8,128)(2,1)} %right_v.1, bf16[4,512,128]{2,1,0:T(8,128)(2,1)} %sketch.1, s32[4,8]{1,0:T(4,128)} %index_hbm.1, ...), custom_call_target="tpu_custom_call" | custom-call | tf_op jit(solution)/shard_map/pallas_call | solution.py:535
  48.8 0.7 %multiply_bitcast_fusion = (f32[4,64,128]{2,1,0:T(8,128)}, f32[4,64,128]{2,1,0:T(8,128)}) fusion(f32[2,4,64,128]{3,2,1,0:T(8,128)S(1)} %shard_map.86), kind=kLoop, calls=%fused_computation | loop fusion | flops 65536 | bytes 524288 | tf_op jit(solution)/shard_map/mul | solution.py:592
